TPU v7x, 32 devices: a whole 2x2x4 slice. The times are simulated.
32 devices in a mesh: shard: 2 (over x), ctx: 4 (over y, core), tp: 4 (over z).
Axes of the slice: x: 2, y: 2, z: 4, core: 2. Of those that a mesh axis runs over, the one named last changes fastest.
Arguments:
- inputs: bfloat16 [2, 2, 4096, 768], P('shard', None, 'ctx'), may hold values from -6 to 6
- lengths: int32 [2, 2], P('shard'), may hold values from 2048 to 4096, as said below
- attn_gain: bfloat16 [768], P('shard'), may hold values from 0.099609375 to 1.8984375
- mlp_gain: bfloat16 [768], P('shard'), may hold values from 0.099609375 to 1.8984375
- qkv_weight: bfloat16 [768, 3, 768], P('shard', None, 'tp'), may hold values from -0.21875 to 0.21875
- attn_weight: bfloat16 [768, 768], P('tp', 'shard'), may hold values from -0.875 to 0.875
- mlp_in_weight: bfloat16 [768, 2, 1152], P('shard', None, 'tp'), may hold values from -0.21875 to 0.21875
- mlp_out_weight: bfloat16 [1152, 768], P('tp', 'shard'), may hold values from -0.1875 to 0.1875
- cotangent: bfloat16 [2, 2, 4096, 768], P('shard', None, 'ctx'), may hold values from -6 to 6
Outputs:
- layer_out: bfloat16 [2, 2, 4096, 768], P('shard', None, 'ctx')
- input_grad: bfloat16 [2, 2, 4096, 768], P('shard', None, 'ctx')
- qkv_grad: float32 [768, 3, 768], P('shard', None, 'tp')
- attn_grad: float32 [768, 768], P('tp', 'shard')
- mlp_in_grad: float32 [768, 2, 1152], P('shard', None, 'tp')
- mlp_out_grad: float32 [1152, 768], P('tp', 'shard')
- attn_gain_grad: float32 [768], P(('shard', 'tp'))
- mlp_gain_grad: float32 [768], P(('shard', 'tp'))
Inputs may be any that keep to these rules, and one draw needn't show every extreme that they name: `lengths`: among the 2 sequences of each index of shard one has length 4096; some sequence has length 2048.
All inputs are finite; a program needn't handle non-finite values.
Results may differ from a plain program's by a relative error of at most 0.017.
Values may be sent and summed in bfloat16 or wider, within the bound.
A program may use at most 192 MiB of HBM per device.

v0:
```python
import math
import jax
import jax.numpy as jnp
from jax import lax
from jax.sharding import PartitionSpec as P

HD = 64
HALF = 64
norm_eps = 1e-05
rope_base = 10000.0
masked_score = -1e30


def padded(cells, sides, width):
    for axis, dim in sides:
        count = lax.axis_size(axis)
        ends = count - 1
        head = lax.slice_in_dim(cells, 0, width, axis=dim)
        tail = lax.slice_in_dim(cells, cells.shape[dim] - width, cells.shape[dim], axis=dim)
        cells = jnp.concatenate(
            [
                lax.ppermute(tail, axis, [(i, (i + 1) % count) for i in range(ends)]),
                cells,
                lax.ppermute(head, axis, [((i + 1) % count, i) for i in range(ends)]),
            ],
            axis=dim,
        )
    return cells


def layer_norm(values, gain_row):
    center = values - jnp.mean(values, axis=-1, keepdims=True)
    variance = jnp.mean(center * center, axis=-1, keepdims=True)
    return center * lax.rsqrt(variance + norm_eps) * gain_row


def rope_tables(positions):
    exponents = jnp.arange(0, HD, 2).astype(jnp.float32) / HD
    inverse = jnp.power(rope_base, -exponents)
    angles = positions[:, None] * inverse[None, :]
    angles = jnp.concatenate([angles, angles], axis=-1)[:, None, :]
    return (jnp.cos(angles), jnp.sin(angles))


def rotate(vector, cosine, sine_table):
    half_size = vector.shape[-1] // 2
    turned = jnp.concatenate([-vector[..., half_size:], vector[..., :half_size]], axis=-1)
    return vector * cosine + turned * sine_table


def geglu(gate_up):
    return jax.nn.gelu(gate_up[..., 0, :], approximate=False) * gate_up[..., 1, :]


def on_device(
    inputs,
    lengths,
    attn_gain,
    mlp_gain,
    qkv_weight,
    attn_weight,
    mlp_in_weight,
    mlp_out_weight,
    cotangent,
):
    gathered = (
        lax.all_gather(qkv_weight, "shard", axis=0, tiled=True),
        lax.all_gather(attn_weight, "shard", axis=1, tiled=True),
        lax.all_gather(mlp_in_weight, "shard", axis=0, tiled=True),
        lax.all_gather(mlp_out_weight, "shard", axis=1, tiled=True),
        lax.all_gather(attn_gain, "shard", axis=0, tiled=True),
        lax.all_gather(mlp_gain, "shard", axis=0, tiled=True),
    )
    qkv_full, attn_full, mlp_in_full, mlp_out_full, attn_gain_low, mlp_gain_low = gathered
    gain_attn = attn_gain_low.astype(jnp.float32)
    gain_mlp = mlp_gain_low.astype(jnp.float32)
    seq_in = inputs[0].astype(jnp.float32)
    batch_count = seq_in.shape[0]
    local_len = seq_in.shape[1]
    tp_width = qkv_full.shape[2]
    local_heads = tp_width // HD
    ext_len = local_len + 2 * HALF
    scaling = 1.0 / math.sqrt(HD)
    query_tile = min(512, local_len)
    tile_count = local_len // query_tile
    key_span = query_tile + 2 * HALF
    ctx_index = lax.axis_index("ctx")
    positions = ctx_index * local_len + jnp.arange(local_len, dtype=jnp.int32)
    seq_lengths = lengths[0]
    valid_rows = (positions[None, :] < seq_lengths[:, None]).astype(jnp.float32)[:, :, None]
    tile_starts = jnp.arange(tile_count, dtype=jnp.int32) * query_tile
    query_pos = (
        ctx_index * local_len
        + tile_starts[:, None]
        + jnp.arange(query_tile, dtype=jnp.int32)[None, :]
    )
    key_pos = (
        ctx_index * local_len
        - HALF
        + tile_starts[:, None]
        + jnp.arange(key_span, dtype=jnp.int32)[None, :]
    )
    distance = query_pos[:, :, None] - key_pos[:, None, :]
    near_keys = (jnp.abs(distance) <= HALF) & (key_pos[:, None, :] >= 0)
    live_keys = (key_pos[None, :, None, :] < seq_lengths[:, None, None, None]) | (distance == 0)[
        None
    ]
    allowed = (near_keys[None] & live_keys)[:, :, None]
    cosine, sine_table = rope_tables(positions.astype(jnp.float32))

    def key_tiles(extended):
        return jnp.stack(
            [
                extended[:, index * query_tile : index * query_tile + key_span]
                for index in range(tile_count)
            ],
            axis=1,
        )

    def untile(tiles):
        total = jnp.zeros((batch_count, ext_len, local_heads, HD), jnp.float32)
        for index in range(tile_count):
            after = ext_len - index * query_tile - key_span
            total = total + jnp.pad(
                tiles[:, index], ((0, 0), (index * query_tile, after), (0, 0), (0, 0))
            )
        return total

    normed_attn, back_norm_attn = jax.vjp(layer_norm, seq_in, gain_attn)
    normed_low = normed_attn.astype(jnp.bfloat16)
    qkv_raw = jnp.einsum("mtd,dcf->mtcf", normed_low, qkv_full, preferred_element_type=jnp.float32)
    heads_raw = qkv_raw.reshape(batch_count, local_len, 3, local_heads, HD)

    def rope_pair(query_raw, key_raw):
        return (rotate(query_raw, cosine, sine_table), rotate(key_raw, cosine, sine_table))

    (query_rot, key_rot), back_rope = jax.vjp(rope_pair, heads_raw[:, :, 0], heads_raw[:, :, 1])
    queries = query_rot.astype(jnp.bfloat16)
    key_value = jnp.stack([key_rot.astype(jnp.bfloat16), heads_raw[:, :, 2].astype(jnp.bfloat16)])
    key_value = key_value.reshape(2, batch_count, local_len, tp_width)
    key_value_ext = padded(key_value, (("ctx", 2),), HALF)
    key_value_ext = key_value_ext.reshape(2, batch_count, ext_len, local_heads, HD)
    keys_tiled = key_tiles(key_value_ext[0])
    values_tiled = key_tiles(key_value_ext[1])
    queries_tiled = queries.reshape(batch_count, tile_count, query_tile, local_heads, HD)

    def masked_scores():
        raw_scores = (
            jnp.einsum(
                "mnqhd,mnkhd->mnhqk", queries_tiled, keys_tiled, preferred_element_type=jnp.float32
            )
            * scaling
        )
        return jnp.where(allowed, raw_scores, masked_score)

    scores = masked_scores()
    top_score = jnp.max(scores, axis=-1, keepdims=True)
    exponent_terms = jnp.exp(scores - top_score)
    denominator = jnp.sum(exponent_terms, axis=-1, keepdims=True)
    soft_low = (exponent_terms / denominator).astype(jnp.bfloat16)
    log_total = top_score + jnp.log(denominator)
    context = jnp.einsum(
        "mnhqk,mnkhd->mnqhd", soft_low, values_tiled, preferred_element_type=jnp.float32
    )
    context_low = context.astype(jnp.bfloat16).reshape(batch_count, local_len, tp_width)
    attn_part = jnp.einsum(
        "mtf,fd->mtd", context_low, attn_full, preferred_element_type=jnp.float32
    )
    attn_out = lax.psum(attn_part, "tp")
    middle = seq_in + attn_out
    normed_mlp, back_norm_mlp = jax.vjp(layer_norm, middle, gain_mlp)
    normed_mlp_low = normed_mlp.astype(jnp.bfloat16)
    gate_up = jnp.einsum(
        "mtd,dcf->mtcf", normed_mlp_low, mlp_in_full, preferred_element_type=jnp.float32
    )
    hidden, back_glu = jax.vjp(geglu, gate_up)
    hidden_low = hidden.astype(jnp.bfloat16)
    mlp_part = jnp.einsum(
        "mtf,fd->mtd", hidden_low, mlp_out_full, preferred_element_type=jnp.float32
    )
    mlp_out = lax.psum(mlp_part.astype(jnp.bfloat16), "tp").astype(jnp.float32)
    layer_out = ((middle + mlp_out) * valid_rows).astype(jnp.bfloat16)[None]
    grad_out = cotangent[0].astype(jnp.float32) * valid_rows
    grad_out_low = grad_out.astype(jnp.bfloat16)
    mlp_out_grad = jnp.einsum(
        "mtf,mtd->fd", hidden_low, grad_out_low, preferred_element_type=jnp.float32
    )
    grad_hidden = jnp.einsum(
        "mtd,fd->mtf", grad_out_low, mlp_out_full, preferred_element_type=jnp.float32
    )
    (grad_gate_up,) = back_glu(grad_hidden)
    grad_gate_low = grad_gate_up.astype(jnp.bfloat16)
    mlp_in_grad = jnp.einsum(
        "mtd,mtcf->dcf", normed_mlp_low, grad_gate_low, preferred_element_type=jnp.float32
    )
    grad_mlp_part = jnp.einsum(
        "mtcf,dcf->mtd", grad_gate_low, mlp_in_full, preferred_element_type=jnp.float32
    )
    grad_normed_mlp = lax.psum(grad_mlp_part, "tp")
    grad_mid_norm, mlp_gain_grad = back_norm_mlp(grad_normed_mlp)
    grad_middle = grad_out + grad_mid_norm
    grad_middle_low = grad_middle.astype(jnp.bfloat16)
    attn_grad = jnp.einsum(
        "mtf,mtd->fd", context_low, grad_middle_low, preferred_element_type=jnp.float32
    )
    grad_context = jnp.einsum(
        "mtd,fd->mtf", grad_middle_low, attn_full, preferred_element_type=jnp.float32
    )
    grad_context = grad_context.astype(jnp.bfloat16).reshape(
        batch_count, tile_count, query_tile, local_heads, HD
    )
    soft_again = jnp.exp(masked_scores() - log_total)
    soft_again_low = soft_again.astype(jnp.bfloat16)
    grad_values = jnp.einsum(
        "mnhqk,mnqhd->mnkhd", soft_again_low, grad_context, preferred_element_type=jnp.float32
    )
    grad_soft = jnp.einsum(
        "mnqhd,mnkhd->mnhqk", grad_context, values_tiled, preferred_element_type=jnp.float32
    )
    row_terms = jnp.sum(soft_again * grad_soft, axis=-1, keepdims=True)
    grad_scores = (soft_again * (grad_soft - row_terms)).astype(jnp.bfloat16)
    grad_queries = (
        jnp.einsum(
            "mnhqk,mnkhd->mnqhd", grad_scores, keys_tiled, preferred_element_type=jnp.float32
        )
        * scaling
    )
    grad_queries = grad_queries.reshape(batch_count, local_len, local_heads, HD)
    grad_keys = (
        jnp.einsum(
            "mnhqk,mnqhd->mnkhd", grad_scores, queries_tiled, preferred_element_type=jnp.float32
        )
        * scaling
    )
    grad_ext = jnp.stack([untile(grad_keys), untile(grad_values)]).reshape(
        2, batch_count, ext_len, tp_width
    )
    rim_pairs = jnp.concatenate([grad_ext[:, :, :HALF], grad_ext[:, :, ext_len - HALF :]], axis=2)
    arrived = padded(rim_pairs, (("ctx", 2),), HALF)
    from_lower = arrived[:, :, :HALF]
    from_upper = arrived[:, :, arrived.shape[2] - HALF :]
    grad_own = grad_ext[:, :, HALF : HALF + local_len]
    grad_own = grad_own + jnp.pad(from_lower, ((0, 0), (0, 0), (0, local_len - HALF), (0, 0)))
    grad_own = grad_own + jnp.pad(from_upper, ((0, 0), (0, 0), (local_len - HALF, 0), (0, 0)))
    grad_key_rot = grad_own[0].reshape(batch_count, local_len, local_heads, HD)
    grad_value_own = grad_own[1].reshape(batch_count, local_len, local_heads, HD)
    grad_query_raw, grad_key_raw = back_rope((grad_queries, grad_key_rot))
    grad_qkv = jnp.stack([grad_query_raw, grad_key_raw, grad_value_own], axis=2)
    grad_qkv_low = grad_qkv.reshape(batch_count, local_len, 3, tp_width).astype(jnp.bfloat16)
    qkv_grad = jnp.einsum(
        "mtd,mtcf->dcf", normed_low, grad_qkv_low, preferred_element_type=jnp.float32
    )
    grad_attn_part = jnp.einsum(
        "mtcf,dcf->mtd", grad_qkv_low, qkv_full, preferred_element_type=jnp.float32
    )
    grad_normed = lax.psum(grad_attn_part, "tp")
    grad_in_norm, attn_gain_grad = back_norm_attn(grad_normed)
    input_grad = (grad_middle + grad_in_norm).astype(jnp.bfloat16)[None]
    partials = (qkv_grad, attn_grad, mlp_in_grad, mlp_out_grad, attn_gain_grad, mlp_gain_grad)
    summed = lax.psum(
        (partials[0], partials[1], partials[2], partials[3], partials[4], partials[5]), "ctx"
    )
    reduced = (
        lax.psum_scatter(summed[0], "shard", scatter_dimension=0, tiled=True),
        lax.psum_scatter(summed[1], "shard", scatter_dimension=1, tiled=True),
        lax.psum_scatter(summed[2], "shard", scatter_dimension=0, tiled=True),
        lax.psum_scatter(summed[3], "shard", scatter_dimension=1, tiled=True),
        lax.psum_scatter(summed[4], "shard", scatter_dimension=0, tiled=True),
        lax.psum_scatter(summed[5], "shard", scatter_dimension=0, tiled=True),
    )
    gain_share = reduced[4].shape[0] // lax.axis_size("tp")
    gain_start = lax.axis_index("tp") * gain_share
    attn_gain_out = lax.dynamic_slice_in_dim(reduced[4], gain_start, gain_share)
    mlp_gain_out = lax.dynamic_slice_in_dim(reduced[5], gain_start, gain_share)
    return (
        layer_out,
        input_grad,
        reduced[0],
        reduced[1],
        reduced[2],
        reduced[3],
        attn_gain_out,
        mlp_gain_out,
    )


def solution(mesh):
    in_specs = (
        P("shard", None, "ctx", None),
        P("shard", None),
        P("shard"),
        P("shard"),
        P("shard", None, "tp"),
        P("tp", "shard"),
        P("shard", None, "tp"),
        P("tp", "shard"),
        P("shard", None, "ctx", None),
    )
    out_specs = (
        P("shard", None, "ctx", None),
        P("shard", None, "ctx", None),
        P("shard", None, "tp"),
        P("tp", "shard"),
        P("shard", None, "tp"),
        P("tp", "shard"),
        P(("shard", "tp")),
        P(("shard", "tp")),
    )
    return jax.shard_map(
        on_device, mesh=mesh, in_specs=in_specs, out_specs=out_specs, check_vma=False
    )
```

profile of v0, /device:TPU:0, one launch (start us, length us, event | category | flops | bytes accessed | tf_op | source)
XLA Modules:
  0.0 1094.5 jit_solution(6729855262283549967)
XLA Ops:
  8.1 5.3 all-gather
  17.6 11.8 %all_gather.19 = bf16[768,3,192]{0,2,1:T(8,128)(2,1)S(1)} all-gather(bf16[384,3,192]{0,2,1:T(8,128)(2,1)S(1)} %copy-done.45), channel_id=1, replica_groups=mesh['shard'=2,'ctx'=4,'tp'=4] {'shard'}, dimensions={0}, use_global_device_ids=true | all-gather | bytes 1327104 | tf_op jit(solution)/shard_map/all_gather | solution.py:67
  60.4 7.3 all_gather.20
  85.1 5.0 fusion.106
  104.9 6.9 all_gather.23
  111.8 12.6 %all_gather.22 = bf16[768,2,288]{0,2,1:T(8,128)(2,1)} all-gather(bf16[384,2,288]{0,2,1:T(8,128)(2,1)} %param.15), channel_id=1, replica_groups=mesh['shard'=2,'ctx'=4,'tp'=4] {'shard'}, dimensions={0}, use_global_device_ids=true | all-gather | bytes 1327104 | tf_op jit(solution)/shard_map/all_gather | solution.py:69
  129.1 194.1 %all-reduce.23.cloned.1.call-done = f32[2,1024,768]{2,1,0:T(8,128)} async-done(((f32[2,1024,768]{2,1,0:T(8,128)}), f32[2,1024,768]{2,1,0:T(8,128)}) %all-reduce.23.cloned.1.call-update) | async-done | bytes 6291472 | tf_op jit(solution)/shard_map/psum | solution.py:169
  332.0 5.1 multiply_bitcast_fusion
  345.3 6.4 convolution_convert_fusion
  353.6 9.3 fusion.103
  363.9 7.7 fusion.96
  371.7 194.6 %all-reduce.27.cloned.1.call-done = f32[2,1024,768]{2,1,0:T(8,128)} async-done(((f32[2,1024,768]{2,1,0:T(8,128)}), f32[2,1024,768]{2,1,0:T(8,128)}) %all-reduce.27.cloned.1.call-update) | async-done | bytes 6291472 | tf_op jit(solution)/shard_map/psum | solution.py:199
  566.3 6.2 multiply_reduce_fusion.1
  572.5 116.8 %all-reduce.25.cloned.1.call-done = bf16[2,1024,768]{2,1,0:T(8,128)(2,1)} async-done(((bf16[2,1024,768]{2,1,0:T(8,128)(2,1)}), bf16[2,1024,768]{2,1,0:T(8,128)(2,1)}) %all-reduce.25.cloned.1.call-update) | async-done | bytes 3145744 | tf_op jit(solution)/shard_map/psum | solution.py:181
  689.3 8.3 fusion.174
  707.5 14.0 %multiply_reduce_fusion = (f32[2,2,3,512]{3,2,1,0:T(4,128)S(1)}, f32[2,2,3,512,640]{4,3,2,1,0:T(8,128)}) fusion(f32[2,2,3,512,640]{4,3,2,1,0:T(8,128)} %copy-done, f32[2,2,3,512]{3,2,1,0:T(4,128)S(1)} %log_add_fusion, bf16[2,1,640,3,64]{2,4,3,1,0:T(8,128)(2,1)} %copy-done.33, bf16[2,1,640,3,64]{2,4,3,1,0:T(8,128)(2,1)} %copy-done.32, ...), kind=kOutput, calls=%fused_computation.1 | convolution fusion | flops 515598336 | bytes 33275904 | tf_op jit(solution)/shard_map/mnqhd,mnkhd->mnhqk/dot_general | solution.py:217
  722.7 7.4 multiply_convert_fusion
  761.0 7.3 convolution_bitcast_fusion
  770.3 25.6 %reduce-scatter.5.cloned.1.call-done = f32[384,3,192]{0,2,1:T(8,128)} async-done(((f32[768,3,192]{0,2,1:T(8,128)}), f32[384,3,192]{0,2,1:T(8,128)}) %reduce-scatter.5.cloned.1.call-update) | async-done | bytes 884752 | tf_op jit(solution)/shard_map/reduce_scatter | solution.py:264
  795.9 225.4 %all-reduce.29.cloned.1.call-done = f32[2,1024,768]{2,1,0:T(8,128)} async-done(((f32[2,1024,768]{2,1,0:T(8,128)}), f32[2,1024,768]{2,1,0:T(8,128)}) %all-reduce.29.cloned.1.call-update) | async-done | bytes 6291472 | tf_op jit(solution)/shard_map/psum | solution.py:256
  1029.1 5.0 all-reduce.16
  1034.2 6.7 all-reduce.14
  1042.1 9.2 fusion.30
  1051.3 30.6 %all-reduce.31.cloned.1.call-done = (f32[384,3,192]{0,2,1:T(8,128)}, f32[192,384]{1,0:T(8,128)}, f32[384,2,288]{0,2,1:T(8,128)}, f32[288,384]{1,0:T(8,128)}) async-done(((f32[384,3,192]{0,2,1:T(8,128)}, f32[192,384]{1,0:T(8,128)}, f32[384,2,288]{0,2,1:T(8,128)}, f32[288,384]{1,0:T(8,128)}), (f32[384,3,192]{0,2,1:T(8,128)}, f32[192,384]{1,0:T(8,128)}, f32[384,2,288]{0,2,1:T(8,128)}, ...) | async-done | bytes 2506768 | tf_op jit(solution)/shard_map/psum | solution.py:260
  (254 shorter events, 150.0 us)
Async XLA Ops:
  7.2 316.0 %all-reduce.23.cloned.1.call-start = ((), (), s32[]{:S(2)}) async-start(), calls=%async_computation.4 | async-start | bytes 12582912 | tf_op jit(solution)/shard_map/psum | solution.py:169
  13.4 15.9 %copy-start.54 = (f32[768]{0:T(1024)}, f32[768]{0:T(1024)S(1)}, u32[]{:S(2)}) copy-start(f32[768]{0:T(1024)S(1)} %reshape.411) | copy-start | bytes 9220
  15.9 16.1 %copy-start.46 = (f32[2,1024]{1,0:T(2,128)}, f32[2,1024]{1,0:T(2,128)S(1)}, u32[]{:S(2)}) copy-start(f32[2,1024]{1,0:T(2,128)S(1)} %broadcast_multiply_fusion.5) | copy-start | bytes 24580
  17.6 14.4 %copy-start.52 = (f32[2,1024]{1,0:T(2,128)}, f32[2,1024]{1,0:T(2,128)S(1)}, u32[]{:S(2)}) copy-start(f32[2,1024]{1,0:T(2,128)S(1)} %fusion.130) | copy-start | bytes 24580
  42.4 25.3 %collective-permute-start.1 = (bf16[2,2,64,192]{2,3,1,0:T(8,128)(2,1)}, bf16[2,2,64,192]{2,3,1,0:T(8,128)(2,1)}, u32[]{:S(2)}, u32[]{:S(2)}) collective-permute-start(bf16[2,2,64,192]{2,3,1,0:T(8,128)(2,1)} %get-tuple-element.43), channel_id=1, source_target_pairs={{4,0},{8,4},{12,8},{5,1},{9,5},{13,9},{6,2},{10,6},{14,10},{7,3},{... | collective-permute-start | bytes 294920 | tf_op jit(solution)/shard_map/ppermute | solution.py:24
  43.7 24.0 %collective-permute-start = (bf16[2,2,64,192]{2,3,1,0:T(8,128)(2,1)}, bf16[2,2,64,192]{2,3,1,0:T(8,128)(2,1)}, u32[]{:S(2)}, u32[]{:S(2)}) collective-permute-start(bf16[2,2,64,192]{2,3,1,0:T(8,128)(2,1)} %get-tuple-element.44), channel_id=1, source_target_pairs={{0,4},{4,8},{8,12},{1,5},{5,9},{9,13},{2,6},{6,10},{10,14},{3,7},{... | collective-permute-start | bytes 294920 | tf_op jit(solution)/shard_map/ppermute | solution.py:22
  73.9 8.9 copy-start.32
  74.0 8.9 copy-start.33
  99.9 466.4 %all-reduce.27.cloned.1.call-start = ((), (), s32[]{:S(2)}) async-start(), calls=%async_computation.6 | async-start | bytes 12582912 | tf_op jit(solution)/shard_map/psum | solution.py:199
  111.8 12.7 %copy-start.34 = (bf16[288,768]{1,0:T(8,128)(2,1)}, bf16[288,768]{1,0:T(8,128)(2,1)S(1)}, u32[]{:S(2)}) copy-start(bf16[288,768]{1,0:T(8,128)(2,1)S(1)} %all_gather.23) | copy-start | bytes 1327108
  344.4 345.0 %all-reduce.25.cloned.1.call-start = ((), (), s32[]{:S(2)}) async-start(), calls=%async_computation.5 | async-start | bytes 6291456 | tf_op jit(solution)/shard_map/psum | solution.py:181
  351.7 418.5 %reduce-scatter.11.cloned.1.call-start = ((), (), s32[]{:S(2)}) async-start(), calls=%async_computation.11 | async-start | bytes 1327104 | tf_op jit(solution)/shard_map/reduce_scatter | solution.py:267
  362.9 407.3 %reduce-scatter.9.cloned.1.call-start = ((), (), s32[]{:S(2)}) async-start(), calls=%async_computation.10 | async-start | bytes 2654208 | tf_op jit(solution)/shard_map/reduce_scatter | solution.py:266
  371.7 398.6 %reduce-scatter.7.cloned.1.call-start = ((), (), s32[]{:S(2)}) async-start(), calls=%async_computation.9 | async-start | bytes 884736 | tf_op jit(solution)/shard_map/reduce_scatter | solution.py:265
  704.1 17.4 %slice-start = ((s8[15728640]{0:T(1024)(128)(4,1)}), s8[3145728]{0:T(1024)(128)(4,1)S(1)}, s32[]{:S(2)}) async-start(s8[15728640]{0:T(1024)(128)(4,1)} %bitcast.348), calls=%async_computation.13 | async-start | bytes 6291456
  707.5 14.0 %slice-start.1 = ((s8[15728640]{0:T(1024)(128)(4,1)}), s8[4194304]{0:T(1024)(128)(4,1)S(1)}, s32[]{:S(2)}) async-start(s8[15728640]{0:T(1024)(128)(4,1)} %bitcast.348), calls=%async_computation.14 | async-start | bytes 8388608
  707.5 14.0 %slice-start.2 = ((s8[15728640]{0:T(1024)(128)(4,1)}), s8[4194304]{0:T(1024)(128)(4,1)S(1)}, s32[]{:S(2)}) async-start(s8[15728640]{0:T(1024)(128)(4,1)} %bitcast.348), calls=%async_computation.15 | async-start | bytes 8388608
  707.5 15.2 %slice-start.3 = ((s8[15728640]{0:T(1024)(128)(4,1)}), s8[4194304]{0:T(1024)(128)(4,1)S(1)}, s32[]{:S(2)}) async-start(s8[15728640]{0:T(1024)(128)(4,1)} %bitcast.348), calls=%async_computation.16 | async-start | bytes 8388608
  743.0 5.6 collective-permute-start.2
  745.6 4.5 collective-permute-start.3
  748.5 47.3 %reduce-scatter.5.cloned.1.call-start = ((), (), s32[]{:S(2)}) async-start(), calls=%async_computation.8 | async-start | bytes 2654208 | tf_op jit(solution)/shard_map/reduce_scatter | solution.py:264
  760.9 260.3 %all-reduce.29.cloned.1.call-start = ((), (), s32[]{:S(2)}) async-start(), calls=%async_computation.7 | async-start | bytes 12582912 | tf_op jit(solution)/shard_map/psum | solution.py:256
  768.3 313.6 %all-reduce.31.cloned.1.call-start = ((), (), s32[]{:S(2)}) async-start(), calls=%async_computation.12 | async-start | bytes 5013504 | tf_op jit(solution)/shard_map/psum | solution.py:260
  795.9 229.3 %copy-start.51 = (f32[2,1024]{1,0:T(2,128)S(1)}, f32[2,1024]{1,0:T(2,128)}, u32[]{:S(2)}) copy-start(f32[2,1024]{1,0:T(2,128)} %copy-done.50) | copy-start | bytes 24580
  (53 other events, 147.5 us)
Sparse Core Ops, SparseCore 0:
  100.0 223.1 all-reduce.22
  344.5 221.7 all-reduce.26
  569.3 120.0 all-reduce.24
  692.0 17.5 reduce-scatter.10
  711.7 28.2 reduce-scatter.8
  748.6 16.0 reduce-scatter.6
  767.6 28.2 reduce-scatter.4
  798.3 222.8 all-reduce.28
  1024.0 57.8 all-reduce.30
where the time goes:
time: 1100 us; the launch traced here: 1090 us
  waiting for transfers between devices  789 us (72%)
  matrix products  88.2 us (8%)
  other arithmetic  76 us (7%)
  blocking collectives  60 us (5%)
  local copies, waits for them, and re-layouts  56.3 us (5%)
  between operations  15.9 us (1%)
    psum x1, waiting for transfers between devices, on_device(): grad_normed = lax.psum(grad_attn_part, 'tp')  225 us
    psum x1, waiting for transfers between devices, on_device(): grad_normed_mlp = lax.psum(grad_mlp_part, 'tp')  195 us
    psum x1, waiting for transfers between devices, on_device(): attn_out = lax.psum(attn_part, 'tp')  194 us
    psum x1, waiting for transfers between devices, on_device(): mlp_out = lax.psum(mlp_part.astype(jnp.bfloat16), 'tp').astype(jnp.float32)  117 us
    psum x1, waiting for transfers between devices, on_device(): lax.psum((partials[0], partials[1], partials[2], partials[3], partials[4]...  30.6 us
    unnamed x137, local copies, waits for them, and re-layouts  29.4 us
    reduce_scatter x1, waiting for transfers between devices, on_device(): lax.psum_scatter(summed[0], 'shard', scatter_dimension=0, tiled=True)  25.6 us
  transfers between devices with their start and end apart: 13, of which 7 were waited for; matrix products, arithmetic and copies ran while one was open for 12% of the time, Pallas kernels for 0%

commit v1 on v0

--- a/solution.py
+++ b/solution.py
@@ -166,7 +166,9 @@
     attn_part = jnp.einsum(
         "mtf,fd->mtd", context_low, attn_full, preferred_element_type=jnp.float32
     )
-    attn_out = lax.psum(attn_part, "tp")
+    attn_out = attn_part
+    for hop in (1, 2):
+        attn_out = attn_out + lax.ppermute(attn_out, "tp", [(dev, dev ^ hop) for dev in range(4)])
     middle = seq_in + attn_out
     normed_mlp, back_norm_mlp = jax.vjp(layer_norm, middle, gain_mlp)
     normed_mlp_low = normed_mlp.astype(jnp.bfloat16)

time: 1100 us -> 1270 us (1.15)
  waiting for transfers between devices: 789 us -> 936 us
  local copies, waits for them, and re-layouts: 56.3 us -> 73.3 us
    ppermute x0 -> x2, waiting for transfers between devices: none -> 376 us  [on_device(): lax.ppermute(attn_out, 'tp', [(dev, dev ^ hop) for dev in range(4)])]
    psum x1 -> x0, waiting for transfers between devices: 194 us -> none  [on_device(): attn_out = lax.psum(attn_part, 'tp')]
    psum x1, waiting for transfers between devices: 225 us -> 199 us  [on_device(): grad_normed = lax.psum(grad_attn_part, 'tp')]
    unnamed x137, local copies, waits for them, and re-layouts: 29.4 us -> 46.4 us
  transfers between devices with their start and end apart: 13 -> 14, of which waited for: 7 -> 8; matrix products, arithmetic and copies ran while one was open for 12% -> 11% of each run, Pallas kernels for 0% -> 0%
where the time goes in v1:
time: 1270 us; the launch traced here: 1260 us
  waiting for transfers between devices  936 us (74%)
  matrix products  82.2 us (6%)
  other arithmetic  80.8 us (6%)
  local copies, waits for them, and re-layouts  73.3 us (6%)
  blocking collectives  59.1 us (5%)
  between operations  17.4 us (1%)
  starting transfers between devices  14.1 us (1%)
    ppermute x2, waiting for transfers between devices, on_device(): lax.ppermute(attn_out, 'tp', [(dev, dev ^ hop) for dev in range(4)])  376 us
    psum x1, waiting for transfers between devices, on_device(): grad_normed = lax.psum(grad_attn_part, 'tp')  199 us
    psum x1, waiting for transfers between devices, on_device(): grad_normed_mlp = lax.psum(grad_mlp_part, 'tp')  196 us
    psum x1, waiting for transfers between devices, on_device(): mlp_out = lax.psum(mlp_part.astype(jnp.bfloat16), 'tp').astype(jnp.float32)  117 us
    unnamed x137, local copies, waits for them, and re-layouts  46.4 us
    psum x1, waiting for transfers between devices, on_device(): lax.psum((partials[0], partials[1], partials[2], partials[3], partials[4]...  26.4 us
  transfers between devices with their start and end apart: 14, of which 8 were waited for; matrix products, arithmetic and copies ran while one was open for 11% of the time, Pallas kernels for 0%

profile of v1, /device:TPU:0, one launch (start us, length us, event | category | flops | bytes accessed | tf_op | source)
XLA Modules:
  0.0 1262.8 jit_solution(16985900919278733898)
XLA Ops:
  8.7 5.2 all-gather
  14.0 13.8 %all_gather.19 = bf16[768,3,192]{0,2,1:T(8,128)(2,1)} all-gather(bf16[384,3,192]{0,2,1:T(8,128)(2,1)} %param.13), channel_id=1, replica_groups=mesh['shard'=2,'ctx'=4,'tp'=4] {'shard'}, dimensions={0}, use_global_device_ids=true | all-gather | bytes 1327104 | tf_op jit(solution)/shard_map/all_gather | solution.py:67
  64.5 7.1 all_gather.20
  102.7 135.6 %collective-permute-done.2 = f32[2,1024,768]{1,2,0:T(8,128)S(1)} collective-permute-done((f32[2,1024,768]{1,2,0:T(8,128)S(1)}, f32[2,1024,768]{1,2,0:T(8,128)S(1)}, u32[]{:S(2)}, u32[]{:S(2)}) %collective-permute-start.2) | collective-permute-done | bytes 6291488 | tf_op jit(solution)/shard_map/ppermute | solution.py:171
  254.0 6.8 all_gather.23
  260.8 10.2 all_gather.22
  274.1 240.6 %collective-permute-done.3 = f32[2,1024,768]{1,2,0:T(8,128)} collective-permute-done((f32[2,1024,768]{1,2,0:T(8,128)}, f32[2,1024,768]{1,2,0:T(8,128)}, u32[]{:S(2)}, u32[]{:S(2)}) %collective-permute-start.3) | collective-permute-done | bytes 6291488 | tf_op jit(solution)/shard_map/ppermute | solution.py:171
  514.7 7.1 fusion.176
  526.8 5.1 multiply_bitcast_fusion
  540.1 5.9 convolution_convert_fusion
  547.9 9.0 fusion.102
  557.8 7.5 fusion.95
  565.5 195.9 %all-reduce.24.cloned.1.call-done = f32[2,1024,768]{1,2,0:T(8,128)} async-done(((f32[2,1024,768]{1,2,0:T(8,128)}), f32[2,1024,768]{1,2,0:T(8,128)}) %all-reduce.24.cloned.1.call-update) | async-done | bytes 6291472 | tf_op jit(solution)/shard_map/psum | solution.py:201
  761.4 6.3 multiply_reduce_fusion.1
  767.7 116.7 %all-reduce.22.cloned.1.call-done = bf16[2,1024,768]{1,2,0:T(8,128)(2,1)} async-done(((bf16[2,1024,768]{1,2,0:T(8,128)(2,1)}), bf16[2,1024,768]{1,2,0:T(8,128)(2,1)}) %all-reduce.22.cloned.1.call-update) | async-done | bytes 3145744 | tf_op jit(solution)/shard_map/psum | solution.py:183
  884.4 8.0 fusion.174
  901.9 13.9 %multiply_reduce_fusion = (f32[2,2,3,512]{3,2,1,0:T(4,128)S(1)}, f32[2,2,3,512,640]{4,3,2,1,0:T(8,128)}) fusion(f32[2,2,3,512,640]{4,3,2,1,0:T(8,128)} %copy-done, f32[2,2,3,512]{3,2,1,0:T(4,128)S(1)} %log_add_fusion, bf16[2,1,640,3,64]{2,4,3,1,0:T(8,128)(2,1)} %copy-done.32, bf16[2,1,640,3,64]{2,4,3,1,0:T(8,128)(2,1)} %copy-done.31, ...), kind=kOutput, calls=%fused_computation.1 | convolution fusion | flops 515598336 | bytes 33275904 | tf_op jit(solution)/shard_map/mnqhd,mnkhd->mnhqk/dot_general | solution.py:219
  917.0 7.4 multiply_convert_fusion
  955.2 7.3 convolution_bitcast_fusion
  969.5 20.3 %reduce-scatter.5.cloned.1.call-done = f32[384,3,192]{0,2,1:T(8,128)} async-done(((f32[768,3,192]{0,2,1:T(8,128)}), f32[384,3,192]{0,2,1:T(8,128)}) %reduce-scatter.5.cloned.1.call-update) | async-done | bytes 884752 | tf_op jit(solution)/shard_map/reduce_scatter | solution.py:266
  989.8 199.2 %all-reduce.26.cloned.1.call-done = f32[2,1024,768]{1,2,0:T(8,128)} async-done(((f32[2,1024,768]{1,2,0:T(8,128)}), f32[2,1024,768]{1,2,0:T(8,128)}) %all-reduce.26.cloned.1.call-update) | async-done | bytes 6291472 | tf_op jit(solution)/shard_map/psum | solution.py:258
  1202.1 6.7 all-reduce.14
  1210.0 8.5 fusion.30
  1223.1 26.4 %all-reduce.28.cloned.1.call-done = (f32[384,3,192]{0,2,1:T(8,128)}, f32[192,384]{1,0:T(8,128)}, f32[384,2,288]{0,2,1:T(8,128)}, f32[288,384]{1,0:T(8,128)}) async-done(((f32[384,3,192]{0,2,1:T(8,128)}, f32[192,384]{1,0:T(8,128)}, f32[384,2,288]{0,2,1:T(8,128)}, f32[288,384]{1,0:T(8,128)}), (f32[384,3,192]{0,2,1:T(8,128)}, f32[192,384]{1,0:T(8,128)}, f32[384,2,288]{0,2,1:T(8,128)}, ...) | async-done | bytes 2506768 | tf_op jit(solution)/shard_map/psum | solution.py:262
  (256 shorter events, 175.0 us)
Async XLA Ops:
  8.0 753.4 %all-reduce.24.cloned.1.call-start = ((), (), s32[]{:S(2)}) async-start(), calls=%async_computation.5 | async-start | bytes 12582912 | tf_op jit(solution)/shard_map/psum | solution.py:201
  14.0 18.5 %copy-start.52 = (f32[768]{0:T(1024)}, f32[768]{0:T(1024)S(1)}, u32[]{:S(2)}) copy-start(f32[768]{0:T(1024)S(1)} %reshape.411) | copy-start | bytes 9220
  31.0 483.7 %copy-start.1 = (bf16[1,2,1024,768]{2,3,1,0:T(8,128)(2,1)}, bf16[1,2,1024,768]{2,3,1,0:T(8,128)(2,1)S(1)}, u32[]{:S(2)}) copy-start(bf16[1,2,1024,768]{2,3,1,0:T(8,128)(2,1)S(1)} %copy.77) | copy-start | bytes 9437188
  46.0 25.5 %collective-permute-start.1 = (bf16[2,2,64,192]{2,3,1,0:T(8,128)(2,1)}, bf16[2,2,64,192]{2,3,1,0:T(8,128)(2,1)}, u32[]{:S(2)}, u32[]{:S(2)}) collective-permute-start(bf16[2,2,64,192]{2,3,1,0:T(8,128)(2,1)} %get-tuple-element.67), channel_id=1, source_target_pairs={{4,0},{8,4},{12,8},{5,1},{9,5},{13,9},{6,2},{10,6},{14,10},{7,3},{... | collective-permute-start | bytes 294920 | tf_op jit(solution)/shard_map/ppermute | solution.py:24
  47.3 24.3 %collective-permute-start = (bf16[2,2,64,192]{2,3,1,0:T(8,128)(2,1)}, bf16[2,2,64,192]{2,3,1,0:T(8,128)(2,1)}, u32[]{:S(2)}, u32[]{:S(2)}) collective-permute-start(bf16[2,2,64,192]{2,3,1,0:T(8,128)(2,1)} %get-tuple-element.68), channel_id=1, source_target_pairs={{0,4},{4,8},{8,12},{1,5},{5,9},{9,13},{2,6},{6,10},{10,14},{3,7},{... | collective-permute-start | bytes 294920 | tf_op jit(solution)/shard_map/ppermute | solution.py:22
  77.8 8.9 copy-start.31
  101.1 143.9 %copy-start.56 = (bf16[384]{0:T(512)(128)(2,1)S(1)}, bf16[384]{0:T(512)(128)(2,1)}, u32[]{:S(2)}) copy-start(bf16[384]{0:T(512)(128)(2,1)} %param.12) | copy-start | bytes 2308
  101.1 137.2 %collective-permute-start.2 = (f32[2,1024,768]{1,2,0:T(8,128)S(1)}, f32[2,1024,768]{1,2,0:T(8,128)S(1)}, u32[]{:S(2)}, u32[]{:S(2)}) collective-permute-start(f32[2,1024,768]{1,2,0:T(8,128)S(1)} %fusion.122), channel_id=1, source_target_pairs={{0,1},{1,0},{2,3},{3,2},{4,5},{5,4},{6,7},{7,6},{8,9},{9,8},{10,11... | collective-permute-start | bytes 18874376 | tf_op jit(solution)/shard_map/ppermute | solution.py:171
  242.4 272.3 %collective-permute-start.3 = (f32[2,1024,768]{1,2,0:T(8,128)}, f32[2,1024,768]{1,2,0:T(8,128)}, u32[]{:S(2)}, u32[]{:S(2)}) collective-permute-start(f32[2,1024,768]{1,2,0:T(8,128)} %add.232), channel_id=1, source_target_pairs={{0,2},{1,3},{2,0},{3,1},{4,6},{5,7},{6,4},{7,5},{8,10},{9,11},{10,... | collective-permute-start | bytes 18874376 | tf_op jit(solution)/shard_map/ppermute | solution.py:171
  260.8 13.3 %copy-start.33 = (bf16[288,768]{1,0:T(8,128)(2,1)}, bf16[288,768]{1,0:T(8,128)(2,1)S(1)}, u32[]{:S(2)}) copy-start(bf16[288,768]{1,0:T(8,128)(2,1)S(1)} %all_gather.23) | copy-start | bytes 1327108
  539.1 345.3 %all-reduce.22.cloned.1.call-start = ((), (), s32[]{:S(2)}) async-start(), calls=%async_computation.4 | async-start | bytes 6291456 | tf_op jit(solution)/shard_map/psum | solution.py:183
  546.1 423.4 %reduce-scatter.11.cloned.1.call-start = ((), (), s32[]{:S(2)}) async-start(), calls=%async_computation.10 | async-start | bytes 1327104 | tf_op jit(solution)/shard_map/reduce_scatter | solution.py:269
  557.0 412.5 %reduce-scatter.9.cloned.1.call-start = ((), (), s32[]{:S(2)}) async-start(), calls=%async_computation.9 | async-start | bytes 2654208 | tf_op jit(solution)/shard_map/reduce_scatter | solution.py:268
  565.3 404.2 %reduce-scatter.7.cloned.1.call-start = ((), (), s32[]{:S(2)}) async-start(), calls=%async_computation.8 | async-start | bytes 884736 | tf_op jit(solution)/shard_map/reduce_scatter | solution.py:267
  898.5 17.3 %slice-start = ((s8[15728640]{0:T(1024)(128)(4,1)}), s8[3145728]{0:T(1024)(128)(4,1)S(1)}, s32[]{:S(2)}) async-start(s8[15728640]{0:T(1024)(128)(4,1)} %bitcast.348), calls=%async_computation.12 | async-start | bytes 6291456
  901.9 13.9 %slice-start.1 = ((s8[15728640]{0:T(1024)(128)(4,1)}), s8[4194304]{0:T(1024)(128)(4,1)S(1)}, s32[]{:S(2)}) async-start(s8[15728640]{0:T(1024)(128)(4,1)} %bitcast.348), calls=%async_computation.13 | async-start | bytes 8388608
  901.9 13.9 %slice-start.2 = ((s8[15728640]{0:T(1024)(128)(4,1)}), s8[4194304]{0:T(1024)(128)(4,1)S(1)}, s32[]{:S(2)}) async-start(s8[15728640]{0:T(1024)(128)(4,1)} %bitcast.348), calls=%async_computation.14 | async-start | bytes 8388608
  901.9 15.1 %slice-start.3 = ((s8[15728640]{0:T(1024)(128)(4,1)}), s8[4194304]{0:T(1024)(128)(4,1)S(1)}, s32[]{:S(2)}) async-start(s8[15728640]{0:T(1024)(128)(4,1)} %bitcast.348), calls=%async_computation.15 | async-start | bytes 8388608
  937.2 6.0 collective-permute-start.4
  939.8 4.5 collective-permute-start.5
  943.2 46.6 %reduce-scatter.5.cloned.1.call-start = ((), (), s32[]{:S(2)}) async-start(), calls=%async_computation.7 | async-start | bytes 2654208 | tf_op jit(solution)/shard_map/reduce_scatter | solution.py:266
  955.1 233.9 %all-reduce.26.cloned.1.call-start = ((), (), s32[]{:S(2)}) async-start(), calls=%async_computation.6 | async-start | bytes 12582912 | tf_op jit(solution)/shard_map/psum | solution.py:258
  962.5 287.0 %all-reduce.28.cloned.1.call-start = ((), (), s32[]{:S(2)}) async-start(), calls=%async_computation.11 | async-start | bytes 5013504 | tf_op jit(solution)/shard_map/psum | solution.py:262
  989.8 203.2 %copy-start.49 = (f32[2,1024]{1,0:T(2,128)S(1)}, f32[2,1024]{1,0:T(2,128)}, u32[]{:S(2)}) copy-start(f32[2,1024]{1,0:T(2,128)} %copy-done.48) | copy-start | bytes 24580
  (52 other events, 151.3 us)
Sparse Core Ops, SparseCore 0:
  539.2 222.0 all-reduce.23
  764.3 120.0 all-reduce.21
  962.6 226.3 all-reduce.25
  1191.6 57.8 all-reduce.27
Sparse Core Ops, SparseCore 1:
  557.0 18.0 reduce-scatter.10
  577.2 28.1 reduce-scatter.8
  943.2 16.0 reduce-scatter.6
  961.6 28.1 reduce-scatter.4
